TPU v7x, 128 devices: a whole 4x4x4 slice. The times are simulated.
128 devices in a mesh: rep: 4 (over z_lo, core), ep: 32 (over y, x, z_hi).
Axes of the slice: x: 4, y: 4, z: 4 (z_hi: 2, z_lo: 2; z = z_hi * 2 + z_lo), core: 2. Of those that a mesh axis runs over, the one named last changes fastest.
Arguments:
- tokens: bfloat16 [16384, 2048], P(('rep', 'ep')), may hold values from -6 to 6
- expert_ids: int32 [16384, 8], P(('rep', 'ep')), may hold values from 0 to 127, as said below
- route_weight: float32 [16384, 8], P(('rep', 'ep')), may hold values from 0.05 to 1
- hot_plan: int32 [32], replicated, may hold values from 0 to 3, as said below
- gate_proj: bfloat16 [128, 2048, 768], P(('rep', 'ep')), may hold values from -0.125 to 0.125
- up_proj: bfloat16 [128, 2048, 768], P(('rep', 'ep')), may hold values from -0.125 to 0.125
- down_proj: bfloat16 [128, 768, 2048], P(('rep', 'ep')), may hold values from -0.21875 to 0.21875
Outputs:
- layer_out: bfloat16 [16384, 2048], P(('rep', 'ep'))
- served_load: float32 [128], replicated
Inputs may be any that keep to these rules, and one draw needn't show every extreme that they name: `expert_ids`: within the rows of one device (aligned blocks of 128 tokens) a hot expert is named at most 16 times and any other expert at most 6 times. Some expert that is not hot is named exactly 6 times in every block, and the hot expert of some column exactly 16 times in every block. Expert hot_plan[c] * 32 + c is the hot expert of column c.
All inputs are finite; a program needn't handle non-finite values.
Results may differ from a plain program's by a relative error of at most 0.0057.
Values may be sent and summed in bfloat16 or wider, within the bound.
No kernel may reach another device: no remote copies, remote signals or barrier semaphores. Data moves between devices by JAX's collectives and lax.ppermute only.
A program may use at most 128 MiB of HBM per device.

v0:
```python
import jax
import jax.numpy as jnp
from jax import lax
from jax.sharding import PartitionSpec as P


def from_root(array, axis, root):
    mine = lax.axis_index(axis) == root
    return lax.psum(jnp.where(mine, array, jnp.zeros_like(array)), axis)


def expert_ffn(slot_rows, gate_mat, up_mat, down_mat):
    layout = slot_rows.shape
    flattened = slot_rows.reshape(-1, layout[-1])
    gate_in = jnp.dot(flattened, gate_mat, preferred_element_type=jnp.float32)
    up_in = jnp.dot(flattened, up_mat, preferred_element_type=jnp.float32)
    hidden = (jax.nn.silu(gate_in) * up_in).astype(jnp.bfloat16)
    result = jnp.dot(hidden, down_mat, preferred_element_type=jnp.float32).astype(jnp.bfloat16)
    return result.reshape(layout)


def local(tokens, expert_ids, route_weight, hot_plan, gate_proj, up_proj, down_proj):
    n_rep = lax.axis_size("rep")
    n_ep = lax.axis_size("ep")
    devices = n_rep * n_ep
    my_row = lax.axis_index("rep")
    my_col = lax.axis_index("ep")
    tok_rows, top_count = expert_ids.shape
    model_width = tokens.shape[1]
    routed = tok_rows * top_count
    cool_cap = max(2, 3 * routed // (4 * devices))
    hot_cap = max(4, 2 * routed // devices)
    flat_ids = expert_ids.reshape(-1)
    expert_range = jnp.arange(devices, dtype=jnp.int32)
    column_range = jnp.arange(n_ep, dtype=jnp.int32)
    one_hot = (flat_ids[:, None] == expert_range[None, :]).astype(jnp.int32)
    own_counts = jnp.sum(one_hot, axis=0, dtype=jnp.int32)
    row_match = (jnp.arange(n_rep, dtype=jnp.int32) == my_row)[:, None]
    placed = jnp.where(row_match, own_counts[None, :], jnp.zeros_like(own_counts)[None, :])
    row_counts = lax.psum(placed, ("rep", "ep"))
    same_column = expert_range[:, None] % n_ep == column_range[None, :]
    same_row = expert_range[:, None] // n_ep == hot_plan[None, :]
    hot_flag = jnp.any(same_column & same_row, axis=1)
    counts = jnp.sum(row_counts, axis=0, dtype=jnp.int32)
    hot_expert = hot_plan * n_ep + column_range
    copy_rows = row_counts[:, hot_expert].reshape(-1)
    served = jnp.where(hot_flag, jnp.zeros_like(counts), counts) + copy_rows
    served_load = served.astype(jnp.float32) / jnp.float32(routed)
    is_hot = jnp.sum(one_hot * hot_flag.astype(jnp.int32)[None, :], axis=1, dtype=jnp.int32) > 0
    ordinal = jnp.sum((jnp.cumsum(one_hot, axis=0) - 1) * one_hot, axis=1)
    home_col = flat_ids % n_ep
    source = jnp.arange(routed, dtype=jnp.int32) // top_count

    def pack_rows(slot, total):
        owners = jnp.zeros((total + 1,), jnp.int32).at[slot].set(source)[:total]
        filled = jnp.zeros((total + 1,), jnp.bool_).at[slot].set(True)[:total]
        return jnp.where(filled[:, None], tokens[owners], jnp.zeros((), jnp.bfloat16))

    home_total = devices * cool_cap
    home_slot = jnp.where(is_hot, home_total, flat_ids * cool_cap + ordinal)
    copy_total = n_ep * hot_cap
    copy_slot = jnp.where(is_hot, home_col * hot_cap + ordinal, copy_total)
    copy_send = pack_rows(copy_slot, copy_total).reshape(n_ep, hot_cap, model_width)
    copied = (
        from_root(gate_proj[0], "rep", hot_plan[my_col]),
        from_root(up_proj[0], "rep", hot_plan[my_col]),
        from_root(down_proj[0], "rep", hot_plan[my_col]),
    )
    copy_done = expert_ffn(
        lax.all_to_all(copy_send, "ep", split_axis=0, concat_axis=0, tiled=True),
        copied[0],
        copied[1],
        copied[2],
    )
    copy_back = lax.all_to_all(copy_done, "ep", split_axis=0, concat_axis=0, tiled=True)
    copy_result = copy_back.reshape(copy_total, model_width)[jnp.minimum(copy_slot, copy_total - 1)]
    home_send = pack_rows(home_slot, home_total).reshape(devices, cool_cap, model_width)
    home_done = expert_ffn(
        lax.all_to_all(home_send, ("rep", "ep"), split_axis=0, concat_axis=0, tiled=True),
        gate_proj[0],
        up_proj[0],
        down_proj[0],
    )
    home_back = lax.all_to_all(home_done, ("rep", "ep"), split_axis=0, concat_axis=0, tiled=True)
    home_result = home_back.reshape(home_total, model_width)[jnp.minimum(home_slot, home_total - 1)]
    gathered = jnp.where(is_hot[:, None], copy_result, home_result)
    shares = route_weight / jnp.sum(route_weight, axis=1, keepdims=True)
    combined = jnp.sum(
        shares[:, :, None] * gathered.reshape(tok_rows, top_count, model_width).astype(jnp.float32),
        axis=1,
    )
    return (combined.astype(jnp.bfloat16), served_load)


def solution(mesh):
    placed = (
        P(("rep", "ep"), None),
        P(("rep", "ep"), None),
        P(("rep", "ep"), None),
        P(),
        P(("rep", "ep"), None, None),
        P(("rep", "ep"), None, None),
        P(("rep", "ep"), None, None),
    )
    return jax.shard_map(
        local, mesh=mesh, in_specs=placed, out_specs=(P(("rep", "ep"), None), P()), check_vma=False
    )
```

profile of v0, /device:TPU:1, one launch (start us, length us, event | category | flops | bytes accessed | tf_op | source)
XLA Modules:
  0.0 456.8 jit_solution(834048434750761366)
XLA Ops:
  7.2 0.0 copy-start
  7.2 0.0 all-reduce.3.cloned.1.call-start
  7.2 1.3 dynamic_slice.2
  9.2 0.0 copy-start.2
  9.2 0.0 copy-start.3
  9.2 3.9 bitcast_select_fusion.1
  13.1 0.0 copy-done.2
  13.1 1.0 copy-done.3
  14.1 3.0 bitcast_select_fusion.2
  17.1 0.0 copy-start.5
  17.1 0.0 all-reduce.3.cloned.1.call-update
  17.2 0.7 copy-done.5
  17.8 0.1 copy.19
  17.9 0.1 eq.80
  18.0 0.1 copy.22
  18.1 0.2 fusion.10
  18.3 0.1 eq.70
  18.4 0.1 reshape.309
  18.6 0.1 copy.23
  18.7 0.0 copy-done.6
  18.7 0.1 fusion.14
  18.8 0.5 convert_reduce_fusion
  19.4 4.3 scatter_custom_fusion.3
  23.8 0.0 copy-done
  23.8 4.4 gather_fusion.2
  28.1 6.3 %gather.28 = bf16[128,6,2048]{2,1,0:T(8,128)(2,1)} reshape(bf16[768,2048]{1,0:T(8,128)(2,1)} %gather_fusion.2) | data formatting | bytes 6291456 | tf_op jit(solution)/shard_map/gather | solution.py:57
  34.4 4.3 scatter_custom_fusion.2
  38.8 0.2 broadcast_in_dim.123
  39.0 4.7 %broadcast_select_fusion = bf16[128,6,2048]{2,1,0:T(8,128)(2,1)} fusion(bf16[128,6,2048]{2,1,0:T(8,128)(2,1)} %gather.28, pred[128,6]{1,0:T(8,128)(4,1)S(1)} %broadcast_in_dim.123), kind=kLoop, calls=%fused_computation.11 | loop fusion | flops 1572864 | bytes 6292224 | tf_op jit(solution)/shard_map/jit(_where)/select_n | solution.py:57
  43.7 11.8 %all-to-all-start.2 = ((bf16[128,6,2048]{2,1,0:T(8,128)(2,1)}), bf16[128,6,2048]{2,1,0:T(8,128)(2,1)}, u32[]{:S(2)}, u32[]{:S(2)}) async-start(bf16[128,6,2048]{2,1,0:T(8,128)(2,1)} %broadcast_select_fusion), calls=%async_computation.2 | async-start | bytes 8388608 | tf_op jit(solution)/shard_map/all_to_all | solution.py:79
  55.6 4.5 scatter_custom_fusion.1
  60.1 4.3 scatter_custom_fusion
  64.4 2.5 gather_fusion
  66.9 0.1 broadcast_in_dim.115
  67.0 1.6 broadcast_select_fusion.1
  68.6 39.2 %all-to-all-done.2 = bf16[128,6,2048]{2,1,0:T(8,128)(2,1)} async-done(((bf16[128,6,2048]{2,1,0:T(8,128)(2,1)}), bf16[128,6,2048]{2,1,0:T(8,128)(2,1)}, u32[]{:S(2)}, u32[]{:S(2)}) %all-to-all-start.2) | async-done | bytes 3145760 | tf_op jit(solution)/shard_map/all_to_all | solution.py:79
  107.8 7.8 %all-to-all-start = ((bf16[32,16,2048]{2,1,0:T(8,128)(2,1)}), bf16[32,16,2048]{2,1,0:T(8,128)(2,1)S(1)}, u32[]{:S(2)}, u32[]{:S(2)}) async-start(bf16[32,16,2048]{2,1,0:T(8,128)(2,1)} %broadcast_select_fusion.1), calls=%async_computation | async-start | bytes 4194304 | tf_op jit(solution)/shard_map/all_to_all | solution.py:70
  115.5 6.4 %reshape.314 = bf16[768,2048]{1,0:T(8,128)(2,1)} reshape(bf16[128,6,2048]{2,1,0:T(8,128)(2,1)} %all-to-all-done.2) | data formatting | bytes 6291456 | tf_op jit(solution)/shard_map/reshape | solution.py:14
  121.9 7.0 %fusion.1 = f32[768,768]{1,0:T(8,128)} fusion(bf16[768,2048]{1,0:T(8,128)(2,1)} %reshape.314, bf16[1,2048,768]{2,1,0:T(8,128)(2,1)} %param.12), kind=kOutput, calls=%fused_computation.15 | convolution fusion | flops 2415919104 | bytes 8650752 | tf_op jit(solution)/shard_map/dot_general | solution.py:16
  128.9 12.0 %convolution_convert_fusion = bf16[768,2048]{1,0:T(8,128)(2,1)} fusion(bf16[1,768,2048]{2,1,0:T(8,128)(2,1)} %param.13, f32[768,768]{1,0:T(8,128)} %fusion.1, bf16[768,2048]{1,0:T(8,128)(2,1)} %reshape.314, bf16[1,2048,768]{2,1,0:T(8,128)(2,1)} %param.11), kind=kOutput, calls=%fused_computation.12 | convolution fusion | flops 4836950016 | bytes 14942208 | tf_op jit(solution)/shard_map/dot_general | solution.py:18
  140.9 6.3 %reshape.315 = bf16[128,6,2048]{2,1,0:T(8,128)(2,1)} reshape(bf16[768,2048]{1,0:T(8,128)(2,1)} %convolution_convert_fusion) | data formatting | bytes 6291456 | tf_op jit(solution)/shard_map/reshape | solution.py:19
  147.2 0.0 all-to-all-done
  147.2 10.1 %all-to-all-start.3 = ((bf16[128,6,2048]{2,1,0:T(8,128)(2,1)}), bf16[128,6,2048]{2,1,0:T(8,128)(2,1)}, u32[]{:S(2)}, u32[]{:S(2)}) async-start(bf16[128,6,2048]{2,1,0:T(8,128)(2,1)} %reshape.315), calls=%async_computation.3 | async-start | bytes 8388608 | tf_op jit(solution)/shard_map/all_to_all | solution.py:84
  157.3 153.7 %all-reduce.3.cloned.1.call-done = (bf16[768,2048]{1,0:T(8,128)(2,1)}, bf16[2048,768]{1,0:T(8,128)(2,1)}, bf16[2048,768]{1,0:T(8,128)(2,1)}) async-done(((bf16[768,2048]{1,0:T(8,128)(2,1)}, bf16[2048,768]{1,0:T(8,128)(2,1)}, bf16[2048,768]{1,0:T(8,128)(2,1)}), (bf16[768,2048]{1,0:T(8,128)(2,1)}, bf16[2048,768]{1,0:T(8,128)(2,1)}, bf16[2048,768]{1,0:T(8,128)(2,1)})) %all-reduce.3.cloned.1.call-update) | async-done | bytes 9437200 | tf_op jit(solution)/shard_map/psum | solution.py:9
  311.0 4.8 %fusion.31 = f32[512,768]{1,0:T(8,128)} fusion(bf16[512,2048]{1,0:T(8,128)(2,1)S(1)} %bitcast.52, bf16[2048,768]{1,0:T(8,128)(2,1)} %get-tuple-element.6), kind=kOutput, calls=%fused_computation.86 | convolution fusion | flops 1610612736 | bytes 6815744 | tf_op jit(solution)/shard_map/dot_general | solution.py:15
  315.8 8.6 %convolution_convert_fusion.1 = bf16[512,2048]{1,0:T(8,128)(2,1)} fusion(bf16[768,2048]{1,0:T(8,128)(2,1)} %get-tuple-element.5, f32[512,768]{1,0:T(8,128)} %fusion.31, bf16[512,2048]{1,0:T(8,128)(2,1)S(1)} %bitcast.53, bf16[2048,768]{1,0:T(8,128)(2,1)} %get-tuple-element.7), kind=kOutput, calls=%fused_computation.21 | convolution fusion | flops 3224633344 | bytes 12058624 | tf_op jit(solution)/shard_map/dot_general | solution.py:18
  324.4 0.0 all-to-all-done.3
  324.4 9.5 %all-to-all-start.1 = ((bf16[32,16,2048]{2,1,0:T(8,128)(2,1)}), bf16[32,16,2048]{2,1,0:T(8,128)(2,1)S(1)}, u32[]{:S(2)}, u32[]{:S(2)}) async-start(bf16[32,16,2048]{2,1,0:T(8,128)(2,1)} %bitcast.51), calls=%async_computation.1 | async-start | bytes 4194304 | tf_op jit(solution)/shard_map/all_to_all | solution.py:75
  333.9 0.1 gt.32
  334.0 0.0 copy-done.4
  334.1 0.1 copy.18
  334.2 0.1 broadcast_select_fusion.2
  334.3 83.8 %psum.31 = s32[4,128]{0,1:T(8,128)S(1)} all-reduce(s32[4,128]{0,1:T(8,128)S(1)} %broadcast_select_fusion.2), channel_id=1, replica_groups=mesh['rep'=4,'ep'=32] {'rep','ep'}, use_global_device_ids=true, to_apply=%region_15.16 | all-reduce | flops 512 | bytes 4096 | tf_op jit(solution)/shard_map/psum | solution.py:40
  418.1 0.1 reduce_sum.62
  418.2 0.6 gather_fusion.4
  418.8 0.1 copy.24
  418.9 0.1 reshape.317
  419.0 0.5 convert_multiply_fusion
  419.5 6.3 %reshape.316 = bf16[768,2048]{1,0:T(8,128)(2,1)} reshape(bf16[128,6,2048]{2,1,0:T(8,128)(2,1)} %all-to-all-done.3) | data formatting | bytes 6291456 | tf_op jit(solution)/shard_map/reshape | solution.py:85
  425.8 11.1 %gather_fusion.3 = bf16[1024,2048]{1,0:T(8,128)(2,1)} fusion(bf16[768,2048]{1,0:T(8,128)(2,1)} %reshape.316, s32[1024]{0:T(1024)S(1)} %broadcast_clamp_fusion), kind=kCustom, calls=%fused_computation.3 | custom fusion | bytes 8392704 | tf_op jit(solution)/shard_map/gather | solution.py:85
  436.9 0.0 all-to-all-done.1
  437.0 6.0 %gather_fusion.1 = bf16[1024,2048]{1,0:T(8,128)(2,1)} fusion(bf16[512,2048]{1,0:T(8,128)(2,1)S(1)} %bitcast.49, s32[1024]{0:T(1024)S(1)} %broadcast_clamp_fusion.1), kind=kCustom, calls=%fused_computation.1 | custom fusion | bytes 8392704 | tf_op jit(solution)/shard_map/gather | solution.py:76
  443.0 7.0 %multiply_reduce_fusion = bf16[128,2048]{1,0:T(8,128)(2,1)} fusion(bf16[1024,2048]{1,0:T(8,128)(2,1)} %gather_fusion.3, bf16[1024,2048]{1,0:T(8,128)(2,1)} %gather_fusion.1, f32[128,8]{1,0:T(8,128)S(1)} %copy.18, pred[128,8]{1,0:T(8,128)(4,1)S(1)} %gt.32), kind=kLoop, calls=%fused_computation.9 | loop fusion | flops 8126464 | bytes 8918016 | tf_op jit(solution)/shard_map/reduce_sum | solution.py:88
  450.0 0.0 copy-done.1
  (27 shorter events, 0.2 us)
Async XLA Ops:
  7.2 16.6 %copy-start = (bf16[128,2048]{1,0:T(8,128)(2,1)S(1)}, bf16[128,2048]{1,0:T(8,128)(2,1)}, u32[]{:S(2)}) copy-start(bf16[128,2048]{1,0:T(8,128)(2,1)} %param.7) | copy-start | bytes 1572868
  7.2 303.8 %all-reduce.3.cloned.1.call-start = ((), (), s32[]{:S(2)}) async-start(), calls=%async_computation.4 | async-start | bytes 18874368 | tf_op jit(solution)/shard_map/psum | solution.py:9
  9.2 3.9 copy-start.2
  9.2 4.9 %copy-start.3 = (bf16[1,2048,768]{2,1,0:T(8,128)(2,1)S(1)}, bf16[1,2048,768]{2,1,0:T(8,128)(2,1)}, u32[]{:S(2)}) copy-start(bf16[1,2048,768]{2,1,0:T(8,128)(2,1)} %param.11) | copy-start | bytes 9437188
  17.1 0.7 copy-start.5
  17.1 1.6 copy-start.6
  43.7 64.1 %all-to-all-start.2 = ((bf16[128,6,2048]{2,1,0:T(8,128)(2,1)}), bf16[128,6,2048]{2,1,0:T(8,128)(2,1)}, u32[]{:S(2)}, u32[]{:S(2)}) async-start(bf16[128,6,2048]{2,1,0:T(8,128)(2,1)} %broadcast_select_fusion), calls=%async_computation.2 | async-start | bytes 8388608 | tf_op jit(solution)/shard_map/all_to_all | solution.py:79
  107.8 39.4 %all-to-all-start = ((bf16[32,16,2048]{2,1,0:T(8,128)(2,1)}), bf16[32,16,2048]{2,1,0:T(8,128)(2,1)S(1)}, u32[]{:S(2)}, u32[]{:S(2)}) async-start(bf16[32,16,2048]{2,1,0:T(8,128)(2,1)} %broadcast_select_fusion.1), calls=%async_computation | async-start | bytes 4194304 | tf_op jit(solution)/shard_map/all_to_all | solution.py:70
  147.2 177.3 %all-to-all-start.3 = ((bf16[128,6,2048]{2,1,0:T(8,128)(2,1)}), bf16[128,6,2048]{2,1,0:T(8,128)(2,1)}, u32[]{:S(2)}, u32[]{:S(2)}) async-start(bf16[128,6,2048]{2,1,0:T(8,128)(2,1)} %reshape.315), calls=%async_computation.3 | async-start | bytes 8388608 | tf_op jit(solution)/shard_map/all_to_all | solution.py:84
  324.4 9.6 %copy-start.4 = (f32[128,8]{0,1:T(8,128)S(1)}, f32[128,8]{0,1:T(8,128)}, u32[]{:S(2)}) copy-start(f32[128,8]{0,1:T(8,128)} %param.9) | copy-start | bytes 12292
  324.4 112.5 %all-to-all-start.1 = ((bf16[32,16,2048]{2,1,0:T(8,128)(2,1)}), bf16[32,16,2048]{2,1,0:T(8,128)(2,1)S(1)}, u32[]{:S(2)}, u32[]{:S(2)}) async-start(bf16[32,16,2048]{2,1,0:T(8,128)(2,1)} %bitcast.51), calls=%async_computation.1 | async-start | bytes 4194304 | tf_op jit(solution)/shard_map/all_to_all | solution.py:75
  436.9 13.0 %copy-start.1 = (bf16[128,2048]{1,0:T(8,128)(2,1)S(1)}, bf16[128,2048]{1,0:T(8,128)(2,1)}, u32[]{:S(2)}) copy-start(bf16[128,2048]{1,0:T(8,128)(2,1)} %param.7) | copy-start | bytes 1572868
Sparse Core Ops, SparseCore 0:
  17.3 293.6 all-reduce.2
where the time goes:
time: 458 us; the launch traced here: 457 us
  waiting for transfers between devices  193 us (42%)
  blocking collectives  83.8 us (18%)
  local copies, waits for them, and re-layouts  71.5 us (16%)
  starting transfers between devices  39.2 us (9%)
  matrix products  32.5 us (7%)
  other arithmetic  21.9 us (5%)
  between operations  15 us (3%)
    psum x1, waiting for transfers between devices, from_root(): return lax.psum(jnp.where(mine, array, jnp.zeros_like(array)), axis)  154 us
    psum x1, blocking collectives, local(): row_counts = lax.psum(placed, ('rep', 'ep'))  83.8 us
    all_to_all x1, waiting for transfers between devices, local(): lax.all_to_all(home_send, ('rep', 'ep'), split_axis=0, concat_axis=0, til...  39.2 us
    dot_general x2, matrix products, expert_ffn(): jnp.dot(hidden, down_mat, preferred_element_type=jnp.float32)  20.7 us
    gather x3, local copies, waits for them, and re-layouts, pack_rows(): tokens[owners]  13.1 us
    all_to_all x1, starting transfers between devices, local(): lax.all_to_all(home_send, ('rep', 'ep'), split_axis=0, concat_axis=0, til...  11.8 us
    gather x1, local copies, waits for them, and re-layouts, local(): home_back.reshape(home_total, model_width)  11.1 us
    all_to_all x1, starting transfers between devices, local(): lax.all_to_all(home_done, ('rep', 'ep'), split_axis=0, concat_axis=0, til...  10.1 us
  transfers between devices with their start and end apart: 5, of which 2 were waited for; matrix products, arithmetic and copies ran while one was open for 23% of the time, Pallas kernels for 0%

commit v1 on v0

--- a/solution.py
+++ b/solution.py
@@ -6,7 +6,7 @@
 
 def from_root(array, axis, root):
     mine = lax.axis_index(axis) == root
-    return lax.psum(jnp.where(mine, array, jnp.zeros_like(array)), axis)
+    return jnp.sum(lax.all_gather(jnp.where(mine, array, jnp.zeros_like(array)), axis), axis=0)
 
 
 def expert_ffn(slot_rows, gate_mat, up_mat, down_mat):

time: 458 us -> 652 us (1.42); the launches traced: 457 us -> 643 us
  waiting for transfers between devices: 193 us -> 345 us
  other arithmetic: 21.9 us -> 54.8 us
    all_gather x0 -> x3, waiting for transfers between devices: none -> 306 us  [from_root(): lax.all_gather(jnp.where(mine, array, jnp.zeros_like(array)), axis)]
    psum x1 -> x0, waiting for transfers between devices: 154 us -> none  [from_root(): return lax.psum(jnp.where(mine, array, jnp.zeros_like(array)), axis)]
    reduce_sum x0 -> x3, other arithmetic: none -> 28.3 us  [from_root(): jnp.sum(lax.all_gather(jnp.where(mine, array, jnp.zeros_like(array)), axi...]
  transfers between devices with their start and end apart: 5 -> 7, of which waited for: 2 -> 4; matrix products, arithmetic and copies ran while one was open for 23% -> 22% of each run, Pallas kernels for 0% -> 0%
where the time goes in v1:
time: 652 us; the launch traced here: 643 us
  waiting for transfers between devices  345 us (53%)
  blocking collectives  85.8 us (13%)
  local copies, waits for them, and re-layouts  70.7 us (11%)
  other arithmetic  54.8 us (8%)
  starting transfers between devices  39 us (6%)
  matrix products  32.5 us (5%)
  between operations  14.9 us (2%)
    all_gather x3, waiting for transfers between devices, from_root(): lax.all_gather(jnp.where(mine, array, jnp.zeros_like(array)), axis)  306 us
    psum x1, blocking collectives, local(): row_counts = lax.psum(placed, ('rep', 'ep'))  85.8 us
    all_to_all x1, waiting for transfers between devices, local(): lax.all_to_all(home_send, ('rep', 'ep'), split_axis=0, concat_axis=0, til...  39 us
    reduce_sum x3, other arithmetic, from_root(): jnp.sum(lax.all_gather(jnp.where(mine, array, jnp.zeros_like(array)), axi...  28.3 us
    dot_general x2, matrix products, expert_ffn(): jnp.dot(hidden, down_mat, preferred_element_type=jnp.float32)  20.8 us
    gather x3, local copies, waits for them, and re-layouts, pack_rows(): tokens[owners]  13.1 us
  transfers between devices with their start and end apart: 7, of which 4 were waited for; matrix products, arithmetic and copies ran while one was open for 22% of the time, Pallas kernels for 0%

profile of v1, /device:TPU:1, one launch (start us, length us, event | category | flops | bytes accessed | tf_op | source)
XLA Modules:
  0.0 642.9 jit_solution(2075141681361748877)
XLA Ops:
  7.2 0.0 copy-start
  7.2 0.0 all-gather.4.cloned.1.call-start
  7.2 1.3 dynamic_slice.2
  9.2 3.8 broadcast_select_fusion.3
  13.0 0.0 all-gather.4.cloned.1.call-update
  13.0 0.0 all-gather.6.cloned.1.call-start
  13.1 3.8 broadcast_select_fusion.2
  16.9 0.0 all-gather.6.cloned.1.call-update
  16.9 0.0 all-gather.8.cloned.1.call-start
  16.9 3.9 broadcast_select_fusion.1
  20.8 0.0 all-gather.8.cloned.1.call-update
  20.8 0.7 copy-done.3
  21.5 0.1 copy.26
  21.6 0.1 eq.80
  21.7 0.1 eq.70
  21.8 0.1 reshape.309
  21.9 0.1 copy.29
  22.0 0.2 fusion.10
  22.3 0.1 copy.30
  22.4 0.1 fusion.14
  22.5 0.5 convert_reduce_fusion
  23.1 4.3 scatter_custom_fusion.3
  27.4 4.3 gather_fusion.2
  31.7 6.3 gather.28
  38.1 4.3 scatter_custom_fusion.2
  42.4 0.2 broadcast_in_dim.123
  42.6 4.8 broadcast_select_fusion
  47.3 11.7 %all-to-all-start.2 = ((bf16[128,6,2048]{2,1,0:T(8,128)(2,1)}), bf16[128,6,2048]{2,1,0:T(8,128)(2,1)}, u32[]{:S(2)}, u32[]{:S(2)}) async-start(bf16[128,6,2048]{2,1,0:T(8,128)(2,1)} %broadcast_select_fusion), calls=%async_computation.2 | async-start | bytes 8388608 | tf_op jit(solution)/shard_map/all_to_all | solution.py:79
  59.0 4.8 scatter_custom_fusion.1
  63.8 4.3 scatter_custom_fusion
  68.2 2.5 gather_fusion
  70.7 0.1 broadcast_in_dim.115
  70.7 1.5 broadcast_select_fusion.4
  72.3 39.0 %all-to-all-done.2 = bf16[128,6,2048]{2,1,0:T(8,128)(2,1)} async-done(((bf16[128,6,2048]{2,1,0:T(8,128)(2,1)}), bf16[128,6,2048]{2,1,0:T(8,128)(2,1)}, u32[]{:S(2)}, u32[]{:S(2)}) %all-to-all-start.2) | async-done | bytes 3145760 | tf_op jit(solution)/shard_map/all_to_all | solution.py:79
  111.2 7.8 %all-to-all-start = ((bf16[32,16,2048]{2,1,0:T(8,128)(2,1)}), bf16[32,16,2048]{2,1,0:T(8,128)(2,1)S(1)}, u32[]{:S(2)}, u32[]{:S(2)}) async-start(bf16[32,16,2048]{2,1,0:T(8,128)(2,1)} %broadcast_select_fusion.4), calls=%async_computation | async-start | bytes 4194304 | tf_op jit(solution)/shard_map/all_to_all | solution.py:70
  119.0 6.3 reshape.314
  125.3 6.9 %fusion.1 = f32[768,768]{1,0:T(8,128)} fusion(bf16[768,2048]{1,0:T(8,128)(2,1)} %reshape.314, bf16[1,2048,768]{2,1,0:T(8,128)(2,1)} %param.12), kind=kOutput, calls=%fused_computation.14 | convolution fusion | flops 2415919104 | bytes 8650752 | tf_op jit(solution)/shard_map/dot_general | solution.py:16
  132.2 12.0 %convolution_convert_fusion = bf16[768,2048]{1,0:T(8,128)(2,1)} fusion(bf16[1,768,2048]{2,1,0:T(8,128)(2,1)} %param.13, f32[768,768]{1,0:T(8,128)} %fusion.1, bf16[768,2048]{1,0:T(8,128)(2,1)} %reshape.314, bf16[1,2048,768]{2,1,0:T(8,128)(2,1)} %param.11), kind=kOutput, calls=%fused_computation.12 | convolution fusion | flops 4836950016 | bytes 14942208 | tf_op jit(solution)/shard_map/dot_general | solution.py:18
  144.2 6.3 reshape.315
  150.4 0.0 all-to-all-done
  150.4 10.2 %all-to-all-start.3 = ((bf16[128,6,2048]{2,1,0:T(8,128)(2,1)}), bf16[128,6,2048]{2,1,0:T(8,128)(2,1)}, u32[]{:S(2)}, u32[]{:S(2)}) async-start(bf16[128,6,2048]{2,1,0:T(8,128)(2,1)} %reshape.315), calls=%async_computation.3 | async-start | bytes 8388608 | tf_op jit(solution)/shard_map/all_to_all | solution.py:84
  160.7 85.5 %all-gather.4.cloned.1.call-done = bf16[4,2048,768]{2,1,0:T(8,128)(2,1)} async-done(((bf16[1,2048,768]{2,1,0:T(8,128)(2,1)}), bf16[4,2048,768]{2,1,0:T(8,128)(2,1)}) %all-gather.4.cloned.1.call-update) | async-done | bytes 12582928 | tf_op jit(solution)/shard_map/all_gather | solution.py:9
  246.2 9.0 %reduce_sum.96 = bf16[2048,768]{1,0:T(8,128)(2,1)} reduce(bf16[4,2048,768]{2,1,0:T(8,128)(2,1)} %all-gather.4.cloned.1.call-done, bf16[]{:T(256)} %constant.114.clone.1), dimensions={0}, to_apply=%region_8.9 | reduce | flops 4718592 | bytes 15728642 | tf_op jit(solution)/shard_map/reduce_sum | solution.py:9
  255.2 110.7 %all-gather.6.cloned.1.call-done = bf16[4,2048,768]{2,1,0:T(8,128)(2,1)} async-done(((bf16[1,2048,768]{2,1,0:T(8,128)(2,1)}), bf16[4,2048,768]{2,1,0:T(8,128)(2,1)}) %all-gather.6.cloned.1.call-update) | async-done | bytes 12582928 | tf_op jit(solution)/shard_map/all_gather | solution.py:9
  366.0 9.0 %reduce_sum.97 = bf16[2048,768]{1,0:T(8,128)(2,1)} reduce(bf16[4,2048,768]{2,1,0:T(8,128)(2,1)} %all-gather.6.cloned.1.call-done, bf16[]{:T(256)} %constant.114.clone.1), dimensions={0}, to_apply=%region_9.10 | reduce | flops 4718592 | bytes 15728642 | tf_op jit(solution)/shard_map/reduce_sum | solution.py:9
  375.0 109.8 %all-gather.8.cloned.1.call-done = bf16[4,768,2048]{2,1,0:T(8,128)(2,1)} async-done(((bf16[1,768,2048]{2,1,0:T(8,128)(2,1)}), bf16[4,768,2048]{2,1,0:T(8,128)(2,1)}) %all-gather.8.cloned.1.call-update) | async-done | bytes 12582928 | tf_op jit(solution)/shard_map/all_gather | solution.py:9
  484.8 10.2 %reduce_sum.98 = bf16[768,2048]{1,0:T(8,128)(2,1)} reduce(bf16[4,768,2048]{2,1,0:T(8,128)(2,1)} %all-gather.8.cloned.1.call-done, bf16[]{:T(256)} %constant.114.clone.1), dimensions={0}, to_apply=%region_10.11 | reduce | flops 4718592 | bytes 15728642 | tf_op jit(solution)/shard_map/reduce_sum | solution.py:9
  495.1 4.8 fusion.31
  499.9 8.9 %convolution_convert_fusion.1 = bf16[512,2048]{1,0:T(8,128)(2,1)} fusion(bf16[768,2048]{1,0:T(8,128)(2,1)} %reduce_sum.98, f32[512,768]{1,0:T(8,128)} %fusion.31, bf16[512,2048]{1,0:T(8,128)(2,1)S(1)} %bitcast.50, bf16[2048,768]{1,0:T(8,128)(2,1)} %reduce_sum.97), kind=kOutput, calls=%fused_computation.21 | convolution fusion | flops 3224633344 | bytes 12058624 | tf_op jit(solution)/shard_map/dot_general | solution.py:18
  508.8 0.0 all-to-all-done.3
  508.8 9.2 %all-to-all-start.1 = ((bf16[32,16,2048]{2,1,0:T(8,128)(2,1)}), bf16[32,16,2048]{2,1,0:T(8,128)(2,1)S(1)}, u32[]{:S(2)}, u32[]{:S(2)}) async-start(bf16[32,16,2048]{2,1,0:T(8,128)(2,1)} %bitcast.48), calls=%async_computation.1 | async-start | bytes 4194304 | tf_op jit(solution)/shard_map/all_to_all | solution.py:75
  518.0 0.1 gt.32
  518.2 0.1 copy.25
  518.3 0.1 broadcast_select_fusion.5
  518.4 85.8 %psum.7 = s32[4,128]{0,1:T(8,128)S(1)} all-reduce(s32[4,128]{0,1:T(8,128)S(1)} %broadcast_select_fusion.5), channel_id=1, replica_groups=mesh['rep'=4,'ep'=32] {'rep','ep'}, use_global_device_ids=true, to_apply=%region_15.16 | all-reduce | flops 512 | bytes 4096 | tf_op jit(solution)/shard_map/psum | solution.py:40
  604.2 0.1 reduce_sum.101
  604.3 0.6 gather_fusion.4
  604.9 0.1 copy.31
  604.9 0.1 reshape.317
  605.0 0.5 convert_multiply_fusion
  605.6 6.3 reshape.316
  611.9 11.1 %gather_fusion.3 = bf16[1024,2048]{1,0:T(8,128)(2,1)} fusion(bf16[768,2048]{1,0:T(8,128)(2,1)} %reshape.316, s32[1024]{0:T(1024)S(1)} %broadcast_clamp_fusion), kind=kCustom, calls=%fused_computation.3 | custom fusion | bytes 8392704 | tf_op jit(solution)/shard_map/gather | solution.py:85
  623.0 6.1 gather_fusion.1
  629.1 7.0 %multiply_reduce_fusion = bf16[128,2048]{1,0:T(8,128)(2,1)} fusion(bf16[1024,2048]{1,0:T(8,128)(2,1)} %gather_fusion.3, bf16[1024,2048]{1,0:T(8,128)(2,1)} %gather_fusion.1, f32[128,8]{1,0:T(8,128)S(1)} %copy.25, pred[128,8]{1,0:T(8,128)(4,1)S(1)} %gt.32), kind=kLoop, calls=%fused_computation.9 | loop fusion | flops 8126464 | bytes 8918016 | tf_op jit(solution)/shard_map/reduce_sum | solution.py:88
  (33 shorter events, 0.2 us)
Async XLA Ops:
  7.2 20.3 %copy-start = (bf16[128,2048]{1,0:T(8,128)(2,1)S(1)}, bf16[128,2048]{1,0:T(8,128)(2,1)}, u32[]{:S(2)}) copy-start(bf16[128,2048]{1,0:T(8,128)(2,1)} %param.7) | copy-start | bytes 1572868
  7.2 239.0 %all-gather.4.cloned.1.call-start = ((), (), s32[]{:S(2)}) async-start(), calls=%async_computation.4 | async-start | bytes 15728640 | tf_op jit(solution)/shard_map/all_gather | solution.py:9
  13.0 352.9 %all-gather.6.cloned.1.call-start = ((), (), s32[]{:S(2)}) async-start(), calls=%async_computation.5 | async-start | bytes 15728640 | tf_op jit(solution)/shard_map/all_gather | solution.py:9
  16.9 468.0 %all-gather.8.cloned.1.call-start = ((), (), s32[]{:S(2)}) async-start(), calls=%async_computation.6 | async-start | bytes 15728640 | tf_op jit(solution)/shard_map/all_gather | solution.py:9
  20.8 0.7 copy-start.3
  20.8 1.6 copy-start.4
  47.3 63.9 %all-to-all-start.2 = ((bf16[128,6,2048]{2,1,0:T(8,128)(2,1)}), bf16[128,6,2048]{2,1,0:T(8,128)(2,1)}, u32[]{:S(2)}, u32[]{:S(2)}) async-start(bf16[128,6,2048]{2,1,0:T(8,128)(2,1)} %broadcast_select_fusion), calls=%async_computation.2 | async-start | bytes 8388608 | tf_op jit(solution)/shard_map/all_to_all | solution.py:79
  111.2 39.2 %all-to-all-start = ((bf16[32,16,2048]{2,1,0:T(8,128)(2,1)}), bf16[32,16,2048]{2,1,0:T(8,128)(2,1)S(1)}, u32[]{:S(2)}, u32[]{:S(2)}) async-start(bf16[32,16,2048]{2,1,0:T(8,128)(2,1)} %broadcast_select_fusion.4), calls=%async_computation | async-start | bytes 4194304 | tf_op jit(solution)/shard_map/all_to_all | solution.py:70
  150.4 358.3 %all-to-all-start.3 = ((bf16[128,6,2048]{2,1,0:T(8,128)(2,1)}), bf16[128,6,2048]{2,1,0:T(8,128)(2,1)}, u32[]{:S(2)}, u32[]{:S(2)}) async-start(bf16[128,6,2048]{2,1,0:T(8,128)(2,1)} %reshape.315), calls=%async_computation.3 | async-start | bytes 8388608 | tf_op jit(solution)/shard_map/all_to_all | solution.py:84
  508.8 9.4 %copy-start.2 = (f32[128,8]{0,1:T(8,128)S(1)}, f32[128,8]{0,1:T(8,128)}, u32[]{:S(2)}) copy-start(f32[128,8]{0,1:T(8,128)} %param.9) | copy-start | bytes 12292
  508.8 114.3 %all-to-all-start.1 = ((bf16[32,16,2048]{2,1,0:T(8,128)(2,1)}), bf16[32,16,2048]{2,1,0:T(8,128)(2,1)S(1)}, u32[]{:S(2)}, u32[]{:S(2)}) async-start(bf16[32,16,2048]{2,1,0:T(8,128)(2,1)} %bitcast.48), calls=%async_computation.1 | async-start | bytes 4194304 | tf_op jit(solution)/shard_map/all_to_all | solution.py:75
  623.0 13.1 %copy-start.1 = (bf16[128,2048]{1,0:T(8,128)(2,1)S(1)}, bf16[128,2048]{1,0:T(8,128)(2,1)}, u32[]{:S(2)}) copy-start(bf16[128,2048]{1,0:T(8,128)(2,1)} %param.7) | copy-start | bytes 1572868
Sparse Core Ops, SparseCore 0:
  13.1 233.0 all-gather.3
  247.9 118.0 all-gather.5
  367.6 117.1 all-gather.7
